TPU v7x, 32 devices: a whole 2x2x4 slice. The times are simulated.
32 devices in a mesh: groups: 2 (over y), seq: 4 (over z), head: 2 (over x), rep: 2 (over core).
Axes of the slice: x: 2, y: 2, z: 4, core: 2. Of those that a mesh axis runs over, the one named last changes fastest.
Arguments:
- tokens: bfloat16 [4096, 5376], P(('groups', 'seq'), ('head', 'rep')), parts along dimension 0, may hold values from -6 to 6
- query_matrix: bfloat16 [5376, 2048], P(None, ('head', 'rep')), may hold values from -0.078125 to 0.078125
- key_matrix: bfloat16 [5376, 1024], P(None, 'head'), may hold values from -0.078125 to 0.078125
- value_matrix: bfloat16 [5376, 1024], P(None, 'head'), may hold values from -0.078125 to 0.078125
- output_matrix: bfloat16 [2048, 5376], P(None, ('head', 'rep')), may hold values from -0.125 to 0.125
- query_gain: float32 [128], replicated, may hold values from 0.1 to 1.9
- key_norm_gain: float32 [128], replicated, may hold values from 0.1 to 1.9
- adapter_down: bfloat16 [8, 5376, 96], P('seq', ('head', 'rep')), may hold values from -0.078125 to 0.078125
- adapter_up_query: bfloat16 [8, 32, 2048], P('seq', None, ('head', 'rep')), may hold values from -1 to 1
- key_value_up_panels: bfloat16 [8, 2, 32, 1024], P('seq', None, None, 'head'), may hold values from -1 to 1
- adapter_out_down: bfloat16 [8, 2048, 32], P('seq', ('head', 'rep')), may hold values from -0.125 to 0.125
- adapter_out_up: bfloat16 [8, 32, 5376], P('seq', None, ('head', 'rep')), may hold values from -1 to 1
- request_of_block: int32 [32], P('groups'), parts along dimension 0, may hold values from 0 to 1, never falling along the last dimension, each value on 1 to 12 neighbouring positions
- adapter_of_request: int32 [4], P('groups'), parts along dimension 0, may hold values from 0 to 7
Outputs:
- result: bfloat16 [4096, 5376], P(('groups', 'seq'), ('head', 'rep')), parts along dimension 0
There are 2 independent parts, one for each index of `groups`. A program takes and returns all parts, laid end to end along the dimension named above; an argument that names none is the same for every part. Nothing has to cross between parts.
Inputs may be any that keep to these rules, and one draw needn't show every extreme that they name: `request_of_block`: never falls from one block to the next; every request has 1 to 12 blocks.
All inputs are finite; a program needn't handle non-finite values.
Results may differ from a plain program's by a relative error of at most 0.014.
Values may be sent and summed in bfloat16 or wider, within the bound.
No kernel may reach another device: no remote copies, remote signals or barrier semaphores. Data moves between devices by JAX's collectives and lax.ppermute only.
A program may use at most 128 MiB of HBM per device.

v0:
```python
import math
import jax
import jax.numpy as jnp
from jax import lax
from jax.sharding import PartitionSpec as P

HEAD_SIZE = 128
ADAPTER_RANK = 32
KEY_WINDOW = 1024
BLOCK = 128
norm_epsilon = 1e-06
rope_base = 10000.0
score_scale = 168.0 ** (-0.5)
adapter_scale = 2.0


def shifted(value, axis, by):
    size = lax.axis_size(axis)
    pairs = [(i, i + by) for i in range(size) if 0 <= i + by < size]
    return lax.ppermute(value, axis, pairs)


def per_head_norm(values, scale_gain):
    mean_square = jnp.mean(values * values, axis=-1, keepdims=True)
    return values * lax.rsqrt(mean_square + norm_epsilon) * scale_gain


def rope_tables(positions, head_dim):
    half_dim = head_dim // 2
    frequency = jnp.power(rope_base, -jnp.arange(half_dim, dtype=jnp.float32) * 2.0 / head_dim)
    angles = positions.astype(jnp.float32)[:, None] * frequency[None, :]
    return (jnp.cos(angles), jnp.sin(angles))


def rotate_feature_pairs(values, cosine_table, sine_values):
    half_dim = values.shape[-1] // 2
    first_half = values[..., :half_dim]
    second_half = values[..., half_dim:]
    cosine_table = cosine_table[:, None, :]
    sine_values = sine_values[:, None, :]
    return jnp.concatenate(
        [
            first_half * cosine_table - second_half * sine_values,
            second_half * cosine_table + first_half * sine_values,
        ],
        axis=-1,
    )


def request_starts(block_requests, all_requests):
    earlier = (all_requests[None, :] < block_requests[:, None]).astype(jnp.int32)
    return jnp.sum(earlier, axis=1) * BLOCK


def per_device(
    tokens,
    query_matrix,
    key_matrix,
    value_matrix,
    output_matrix,
    query_gain,
    key_norm_gain,
    adapter_down,
    adapter_up_query,
    key_value_up_panels,
    adapter_out_down,
    adapter_out_up,
    request_of_block,
    adapter_of_request,
):
    tok_rows, width_part = tokens.shape
    query_cols = query_matrix.shape[1]
    key_cols = key_matrix.shape[1]
    query_heads = query_cols // HEAD_SIZE
    block_count = tok_rows // BLOCK
    all_blocks = request_of_block.shape[0]
    request_total = adapter_of_request.shape[0]
    seq_index = lax.axis_index("seq")
    rep_index = lax.axis_index("rep")
    first_row = seq_index * tok_rows
    own_requests = lax.dynamic_slice_in_dim(
        request_of_block, seq_index * block_count, block_count, 0
    )
    request_match = own_requests[:, None] == jnp.arange(request_total, dtype=jnp.int32)[None, :]
    own_adapters = jnp.sum(jnp.where(request_match, adapter_of_request[None, :], 0), axis=1)
    pool_part = (
        lax.all_gather(adapter_down, "seq", axis=0, tiled=True),
        lax.all_gather(adapter_up_query, "seq", axis=0, tiled=True),
        lax.all_gather(key_value_up_panels, "seq", axis=0, tiled=True),
        lax.all_gather(adapter_out_down, "seq", axis=0, tiled=True),
        lax.all_gather(adapter_out_up, "seq", axis=0, tiled=True),
    )
    held_count = pool_part[0].shape[0]
    select = (own_adapters[:, None] == jnp.arange(held_count, dtype=jnp.int32)[None, :]).astype(
        jnp.bfloat16
    )
    (
        picked_down_panels,
        picked_query_panels,
        picked_key_panels,
        chosen_out_down,
        picked_output_up,
    ) = tuple(
        (
            jnp.einsum(
                "bn,n...->b...", select, panel_part, preferred_element_type=jnp.float32
            ).astype(jnp.bfloat16)
            for panel_part in pool_part
        )
    )
    token_block_list = tokens.reshape(block_count, BLOCK, width_part)
    partial_low = jnp.einsum(
        "myj,mjc->myc", token_block_list, picked_down_panels, preferred_element_type=jnp.float32
    ).reshape(tok_rows, 3 * ADAPTER_RANK)
    reduced_rank_rows = (
        lax.psum(partial_low, ("head", "rep"))
        .astype(jnp.bfloat16)
        .reshape(block_count, BLOCK, 3 * ADAPTER_RANK)
    )
    feature_part = lax.all_gather(tokens, ("head", "rep"), axis=1, tiled=True)
    query_add = jnp.dot(feature_part, query_matrix, preferred_element_type=jnp.float32)
    key_add = jnp.dot(feature_part, key_matrix, preferred_element_type=jnp.float32)
    value_add = jnp.dot(feature_part, value_matrix, preferred_element_type=jnp.float32)
    query_linear = query_add
    key_linear = key_add
    value_linear = value_add
    query_linear = query_linear + adapter_scale * jnp.einsum(
        "tlq,tqo->tlo",
        reduced_rank_rows[..., :ADAPTER_RANK],
        picked_query_panels,
        preferred_element_type=jnp.float32,
    ).reshape(tok_rows, query_cols)
    key_linear = key_linear + adapter_scale * jnp.einsum(
        "tlq,tqo->tlo",
        reduced_rank_rows[..., ADAPTER_RANK : 2 * ADAPTER_RANK],
        picked_key_panels[:, 0],
        preferred_element_type=jnp.float32,
    ).reshape(tok_rows, key_cols)
    value_linear = value_linear + adapter_scale * jnp.einsum(
        "tlq,tqo->tlo",
        reduced_rank_rows[..., 2 * ADAPTER_RANK :],
        picked_key_panels[:, 1],
        preferred_element_type=jnp.float32,
    ).reshape(tok_rows, key_cols)
    key_full = key_linear.astype(jnp.bfloat16)
    value_full = value_linear.astype(jnp.bfloat16)
    key_heads = key_cols // HEAD_SIZE
    token_index = first_row + jnp.arange(tok_rows, dtype=jnp.int32)
    token_request = jnp.repeat(own_requests, BLOCK)
    token_start = jnp.repeat(request_starts(own_requests, request_of_block), BLOCK)
    cosine_table, sine_values = rope_tables(token_index - token_start, HEAD_SIZE)
    query_rows = (
        rotate_feature_pairs(
            per_head_norm(query_linear.reshape(tok_rows, query_heads, HEAD_SIZE), query_gain),
            cosine_table,
            sine_values,
        )
        * score_scale
    ).astype(jnp.bfloat16)
    rotated_keys = rotate_feature_pairs(
        per_head_norm(
            key_full.astype(jnp.float32).reshape(tok_rows, key_heads, HEAD_SIZE), key_norm_gain
        ),
        cosine_table,
        sine_values,
    ).astype(jnp.bfloat16)
    group_heads = max(query_heads // 2, 1)
    group_size = query_heads // group_heads
    head_first = rep_index * query_heads // 2
    keys_used = lax.dynamic_slice_in_dim(rotated_keys, head_first, group_heads, 1).reshape(
        tok_rows, group_heads * HEAD_SIZE
    )
    values_used = lax.dynamic_slice_in_dim(
        value_full.reshape(tok_rows, key_heads, HEAD_SIZE), head_first, group_heads, 1
    ).reshape(tok_rows, group_heads * HEAD_SIZE)
    query_groups = query_rows.reshape(tok_rows, group_heads, group_size, HEAD_SIZE)
    block_table = jnp.arange(all_blocks, dtype=jnp.int32)
    empty_state = (
        jnp.zeros((tok_rows, group_heads, group_size, HEAD_SIZE), jnp.float32),
        jnp.zeros((group_heads, group_size, tok_rows), jnp.float32),
    )
    reach_blocks = KEY_WINDOW // tok_rows
    stacked = jnp.stack((keys_used, values_used))
    earlier = []
    for step_back in range(reach_blocks, 0, -1):
        earlier.append(shifted(stacked, "seq", step_back))
    window_stack = jnp.concatenate(earlier + [stacked], axis=1)
    fold_state = empty_state
    offset = first_row - reach_blocks * tok_rows
    key_block = window_stack[0]
    value_block = window_stack[1]
    key_length = key_block.shape[0]
    step_length = math.gcd(key_length, 512)
    steps_count = key_length // step_length
    key_steps = key_block.reshape(steps_count, step_length, group_heads, HEAD_SIZE)
    value_steps = value_block.reshape(steps_count, step_length, group_heads, HEAD_SIZE)

    def one_step(carry_state, step_inputs):
        step_keys, step_values, step_index = step_inputs
        key_position = offset + step_index * step_length + jnp.arange(step_length, dtype=jnp.int32)
        key_block_id = jnp.clip(key_position, 0, all_blocks * BLOCK - 1) // BLOCK
        key_request = jnp.sum(
            jnp.where(key_block_id[:, None] == block_table[None, :], request_of_block[None, :], 0),
            axis=1,
        )
        distance = token_index[:, None] - key_position[None, :]
        allowed = (
            (key_position[None, :] >= 0)
            & (distance >= 0)
            & (distance < KEY_WINDOW)
            & (token_request[:, None] == key_request[None, :])
        )
        scores = jnp.einsum(
            "tcpd,kcd->cptk", query_groups, step_keys, preferred_element_type=jnp.float32
        )
        weights = jnp.where(allowed[None, None], jnp.exp(scores), 0.0)
        numerator, denominator = carry_state
        denominator = denominator + jnp.sum(weights, axis=-1)
        numerator = numerator + jnp.einsum(
            "cptk,kcd->tcpd",
            weights.astype(jnp.bfloat16),
            step_values,
            preferred_element_type=jnp.float32,
        )
        return ((numerator, denominator), None)

    fold_state, unused_out = lax.scan(
        one_step, fold_state, (key_steps, value_steps, jnp.arange(steps_count, dtype=jnp.int32))
    )
    numerator, denominator = fold_state
    attention_result = (
        (numerator / jnp.transpose(denominator, (2, 0, 1))[..., None])
        .astype(jnp.bfloat16)
        .reshape(tok_rows, query_cols)
    )
    output_zero = (
        jnp.zeros((tok_rows, width_part), jnp.float32),
        jnp.zeros((tok_rows, ADAPTER_RANK), jnp.float32),
    )
    projected_rows = jnp.dot(
        lax.all_gather(attention_result, ("head", "rep"), axis=1, tiled=True),
        output_matrix,
        preferred_element_type=jnp.float32,
    )
    projected_rows, lowered = (projected_rows, output_zero[1])
    local_low = jnp.einsum(
        "bkc,bcr->bkr",
        attention_result.reshape(block_count, BLOCK, query_cols),
        chosen_out_down,
        preferred_element_type=jnp.float32,
    ).reshape(tok_rows, ADAPTER_RANK)
    output_reduced_rank = lax.psum(local_low, ("head", "rep")).astype(jnp.bfloat16)
    result = projected_rows + adapter_scale * jnp.einsum(
        "zch,zhp->zcp",
        output_reduced_rank.reshape(block_count, BLOCK, ADAPTER_RANK),
        picked_output_up,
        preferred_element_type=jnp.float32,
    ).reshape(tok_rows, width_part)
    return result.astype(jnp.bfloat16)


def solution(mesh):
    return jax.shard_map(
        per_device,
        mesh=mesh,
        in_specs=(
            P(("groups", "seq"), ("head", "rep")),
            P(None, ("head", "rep")),
            P(None, "head"),
            P(None, "head"),
            P(None, ("head", "rep")),
            P(),
            P(),
            P("seq", ("head", "rep"), None),
            P("seq", None, ("head", "rep")),
            P("seq", None, None, "head"),
            P("seq", ("head", "rep"), None),
            P("seq", None, ("head", "rep")),
            P("groups"),
            P("groups"),
        ),
        out_specs=P(("groups", "seq"), ("head", "rep")),
        check_vma=False,
    )
```

profile of v0, /device:TPU:0, one launch (start us, length us, event | category | flops | bytes accessed | tf_op | source)
XLA Modules:
  0.0 259.6 jit_solution(15790281969873115158)
XLA Ops:
  6.5 0.7 all-gather.6.cloned.1.call-update
  7.3 0.7 all-gather.4.cloned.1.call-update
  8.1 0.8 dynamic_slice.29
  8.9 16.8 %all_gather.24 = bf16[8,32,512]{2,1,0:T(8,128)(2,1)S(1)} all-gather(bf16[2,32,512]{2,1,0:T(8,128)(2,1)} %param.24), channel_id=1, replica_groups=mesh['groups'=2,'seq'=4,'head'=2,'rep'=2] {'seq'}, dimensions={0}, use_global_device_ids=true | all-gather | bytes 327680 | tf_op jit(solution)/shard_map/all_gather | solution.py:88
  25.8 0.8 convert_reduce_fusion
  26.6 0.7 fusion.62
  27.3 23.4 %all_gather.23 = bf16[8,2,32,512]{3,2,1,0:T(8,128)(2,1)S(1)} all-gather(bf16[2,2,32,512]{3,2,1,0:T(8,128)(2,1)} %param.25), channel_id=1, replica_groups=mesh['groups'=2,'seq'=4,'head'=2,'rep'=2] {'seq'}, dimensions={0}, use_global_device_ids=true | all-gather | bytes 655360 | tf_op jit(solution)/shard_map/all_gather | solution.py:89
  50.9 0.5 multiply_cosine_fusion
  51.4 0.4 convolution_convert_fusion.2
  51.9 0.3 convolution_convert_fusion.4
  52.2 15.6 %all-gather.6.cloned.1.call-done = bf16[8,1344,96]{1,2,0:T(8,128)(2,1)} async-done(((bf16[2,1344,96]{1,2,0:T(8,128)(2,1)}), bf16[8,1344,96]{1,2,0:T(8,128)(2,1)}) %all-gather.6.cloned.1.call-update) | async-done | bytes 2064400 | tf_op jit(solution)/shard_map/all_gather | solution.py:87
  67.8 2.6 convolution_convert_fusion
  70.4 0.5 fusion.35
  70.9 16.8 %all-reduce.1 = bf16[512,96]{0,1:T(8,128)(2,1)S(1)} all-reduce(f32[512,96]{0,1:T(8,128)S(1)} %bitcast.140), channel_id=1, replica_groups=mesh['groups'=2,'seq'=4,'head'=2,'rep'=2] {'head','rep'}, use_global_device_ids=true, to_apply=%region_1.2 | all-reduce | flops 49152 | bytes 294912 | tf_op jit(solution)/shard_map/psum | solution.py:116
  87.8 0.3 convolution_multiply_fusion.3
  88.2 1.3 copy.113
  89.5 0.3 convolution_multiply_fusion.1
  89.8 0.3 copy.96
  90.1 0.3 convolution_multiply_fusion.2
  90.5 0.3 copy.91
  90.8 21.5 %all-gather.4.cloned.1.call-done = bf16[512,5376]{0,1:T(8,128)(2,1)} async-done(((bf16[512,1344]{0,1:T(8,128)(2,1)}), bf16[512,5376]{0,1:T(8,128)(2,1)}) %all-gather.4.cloned.1.call-update) | async-done | bytes 5505040 | tf_op jit(solution)/shard_map/all_gather | solution.py:120
  112.4 7.6 %fusion.39 = (f32[512,4]{0,1:T(4,128)S(1)}, bf16[512,512]{0,1:T(8,128)(2,1)S(1)}) fusion(f32[512,512]{0,1:T(8,128)} %copy.113, bf16[512,5376]{0,1:T(8,128)(2,1)} %all-gather.4.cloned.1.call-done, bf16[5376,512]{1,0:T(8,128)(2,1)} %param.18), kind=kOutput, calls=%fused_computation.63 | convolution fusion | flops 2819880960 | bytes 12591104 | tf_op jit(solution)/shard_map/dot_general | solution.py:122
  120.1 5.2 %multiply_reduce_fusion = (f32[512,4]{0,1:T(4,128)S(1)}, f32[512,512]{0,1:T(8,128)S(1)}) fusion(f32[512,512]{0,1:T(8,128)S(1)} %copy.96, bf16[512,5376]{0,1:T(8,128)(2,1)S(1)} %copy-done.7, bf16[5376,512]{1,0:T(8,128)(2,1)} %param.17), kind=kOutput, calls=%fused_computation.69 | convolution fusion | flops 2819356672 | bytes 13115392 | tf_op jit(solution)/shard_map/dot_general | solution.py:121
  125.5 0.2 multiply_multiply_fusion
  125.7 1.1 multiply_subtract_fusion
  126.8 3.0 %fusion.34 = bf16[512,512]{0,1:T(8,128)(2,1)S(1)} fusion(f32[512,512]{0,1:T(8,128)S(1)} %copy.91, bf16[512,5376]{0,1:T(8,128)(2,1)S(1)} %copy-done.7, bf16[5376,512]{1,0:T(8,128)(2,1)S(1)} %bitcast.145), kind=kOutput, calls=%fused_computation.56 | convolution fusion | flops 2819096576 | bytes 12582912 | tf_op jit(solution)/shard_map/dot_general | solution.py:123
  130.2 0.9 pad_maximum_fusion
  131.1 4.3 %collective-permute-start = (bf16[2,512,256]{2,1,0:T(8,128)(2,1)}, bf16[2,512,256]{2,1,0:T(8,128)(2,1)}, u32[]{:S(2)}, u32[]{:S(2)}) collective-permute-start(bf16[2,512,256]{2,1,0:T(8,128)(2,1)} %pad_maximum_fusion), channel_id=1, source_target_pairs={{0,8},{4,12},{1,9},{5,13},{2,10},{6,14},{3,11},{7,15},{16,24},{20,... | collective-permute-start | bytes 1572872 | tf_op jit(solution)/shard_map/ppermute | solution.py:20
  135.5 3.9 %collective-permute-start.1 = (bf16[2,512,256]{2,1,0:T(8,128)(2,1)}, bf16[2,512,256]{2,1,0:T(8,128)(2,1)}, u32[]{:S(2)}, u32[]{:S(2)}) collective-permute-start(bf16[2,512,256]{2,1,0:T(8,128)(2,1)} %pad_maximum_fusion), channel_id=1, source_target_pairs={{0,4},{4,8},{8,12},{1,5},{5,9},{9,13},{2,6},{6,10},{10,14},{3,7},{... | collective-permute-start | bytes 1572872 | tf_op jit(solution)/shard_map/ppermute | solution.py:20
  139.4 0.3 copy.97
  139.7 1.4 copy.98
  141.1 1.1 fusion.41
  142.3 5.1 %collective-permute-done = bf16[2,512,256]{2,1,0:T(8,128)(2,1)} collective-permute-done((bf16[2,512,256]{2,1,0:T(8,128)(2,1)}, bf16[2,512,256]{2,1,0:T(8,128)(2,1)}, u32[]{:S(2)}, u32[]{:S(2)}) %collective-permute-start) | collective-permute-done | bytes 524320 | tf_op jit(solution)/shard_map/ppermute | solution.py:20
  147.3 10.6 %collective-permute-done.1 = bf16[2,512,256]{2,1,0:T(8,128)(2,1)} collective-permute-done((bf16[2,512,256]{2,1,0:T(8,128)(2,1)}, bf16[2,512,256]{2,1,0:T(8,128)(2,1)}, u32[]{:S(2)}, u32[]{:S(2)}) %collective-permute-start.1) | collective-permute-done | bytes 524320 | tf_op jit(solution)/shard_map/ppermute | solution.py:20
  157.9 1.4 maximum_maximum_fusion
  159.4 0.2 reshape_squeeze.6
  159.6 0.2 reshape_squeeze.7
  159.9 29.6 %while.15 = (s32[]{:T(128)}, f32[512,2,2,128]{0,3,2,1:T(8,128)S(1)}, f32[2,2,512]{2,1,0:T(2,128)S(1)}, bf16[3,512,2,128]{3,2,1,0:T(2,128)(2,1)S(1)}, s32[3]{0:T(...) while((s32[]{:T(128)}, ...), condition=%wide.region_8.9_spmd.clone, body=%wide.region_5.8_spmd.clone.sunk | while | flops 543460864 | bytes 13948180 | solution.py:227
  159.9 0.6 dynamic_slice.49
  161.4 0.5 fusion.92
  161.9 0.4 constant_dynamic-slice_fusion.4
  162.3 4.0 %fusion.93 = (f32[2,2,512]{2,1,0:T(2,128)S(1)}, f32[2,512,512,2]{2,1,3,0:T(8,128)}) fusion(pred[512,512]{0,1:T(8,128)(4,1)S(1)} %fusion.92, bf16[512,2,2,128]{3,0,2,1:T(8,128)(2,1)} %get-tuple-element.399, bf16[1,512,2,128]{3,2,1,0:T(2,128)(2,1)S(1)} %get-tuple-element.359), kind=kOutput, calls=%fused_computation.4.clone.1 | convolution fusion | flops 270530560 | bytes 5251072 | tf_op jit(solution)/shard_map/while/body/eval_jaxpr/tcpd,kcd->cptk/dot_general | solution.py:213
  166.3 0.2 copy.178
  166.5 3.2 %fusion.94 = f32[512,2,2,128]{0,3,2,1:T(8,128)S(1)} fusion(f32[2,512,512,2]{2,1,3,0:T(8,128)} %get-tuple-element.360, pred[512,512]{0,1:T(8,128)(4,1)S(1)} %fusion.92, f32[512,2,2,128]{0,3,2,1:T(8,128)S(1)} %get-tuple-element.378, pred[]{:T(512)S(6)} %compare.16, bf16[1,512,2,128]{1,3,2,0:T(8,128)(2,1)S(1)} %copy.178), kind=kOutput, calls=%fused_computation.12.clone.1 | convolution fusion | flops 271056896 | bytes 6815745 | tf_op jit(solution)/shard_map/while/body/eval_jaxpr/cptk,kcd->tcpd/dot_general | solution.py:219
  169.8 0.7 dynamic_slice.49
  171.3 0.5 fusion.92
  171.8 0.4 constant_dynamic-slice_fusion.4
  172.1 4.1 %fusion.93 = (f32[2,2,512]{2,1,0:T(2,128)S(1)}, f32[2,512,512,2]{2,1,3,0:T(8,128)}) fusion(pred[512,512]{0,1:T(8,128)(4,1)S(1)} %fusion.92, bf16[512,2,2,128]{3,0,2,1:T(8,128)(2,1)} %get-tuple-element.399, bf16[1,512,2,128]{3,2,1,0:T(2,128)(2,1)S(1)} %get-tuple-element.359), kind=kOutput, calls=%fused_computation.4.clone.1 | convolution fusion | flops 270530560 | bytes 5251072 | tf_op jit(solution)/shard_map/while/body/eval_jaxpr/tcpd,kcd->cptk/dot_general | solution.py:213
  176.2 0.2 copy.178
  176.4 3.2 %fusion.94 = f32[512,2,2,128]{0,3,2,1:T(8,128)S(1)} fusion(f32[2,512,512,2]{2,1,3,0:T(8,128)} %get-tuple-element.360, pred[512,512]{0,1:T(8,128)(4,1)S(1)} %fusion.92, f32[512,2,2,128]{0,3,2,1:T(8,128)S(1)} %get-tuple-element.378, pred[]{:T(512)S(6)} %compare.16, bf16[1,512,2,128]{1,3,2,0:T(8,128)(2,1)S(1)} %copy.178), kind=kOutput, calls=%fused_computation.12.clone.1 | convolution fusion | flops 271056896 | bytes 6815745 | tf_op jit(solution)/shard_map/while/body/eval_jaxpr/cptk,kcd->tcpd/dot_general | solution.py:219
  179.7 0.7 dynamic_slice.49
  181.2 0.5 fusion.92
  181.7 0.4 constant_dynamic-slice_fusion.4
  182.0 4.1 %fusion.93 = (f32[2,2,512]{2,1,0:T(2,128)S(1)}, f32[2,512,512,2]{2,1,3,0:T(8,128)}) fusion(pred[512,512]{0,1:T(8,128)(4,1)S(1)} %fusion.92, bf16[512,2,2,128]{3,0,2,1:T(8,128)(2,1)} %get-tuple-element.399, bf16[1,512,2,128]{3,2,1,0:T(2,128)(2,1)S(1)} %get-tuple-element.359), kind=kOutput, calls=%fused_computation.4.clone.1 | convolution fusion | flops 270530560 | bytes 5251072 | tf_op jit(solution)/shard_map/while/body/eval_jaxpr/tcpd,kcd->cptk/dot_general | solution.py:213
  186.3 3.2 %fusion.94 = f32[512,2,2,128]{0,3,2,1:T(8,128)S(1)} fusion(f32[2,512,512,2]{2,1,3,0:T(8,128)} %get-tuple-element.360, pred[512,512]{0,1:T(8,128)(4,1)S(1)} %fusion.92, f32[512,2,2,128]{0,3,2,1:T(8,128)S(1)} %get-tuple-element.378, pred[]{:T(512)S(6)} %compare.16, bf16[1,512,2,128]{1,3,2,0:T(8,128)(2,1)S(1)} %copy.178), kind=kOutput, calls=%fused_computation.12.clone.1 | convolution fusion | flops 271056896 | bytes 6815745 | tf_op jit(solution)/shard_map/while/body/eval_jaxpr/cptk,kcd->tcpd/dot_general | solution.py:219
  189.6 0.9 divide_convert_fusion
  190.5 26.5 %all_gather.26 = bf16[8,512,32]{1,2,0:T(8,128)(2,1)S(1)} all-gather(bf16[2,512,32]{1,2,0:T(8,128)(2,1)S(1)} %copy-done.3), channel_id=1, replica_groups=mesh['groups'=2,'seq'=4,'head'=2,'rep'=2] {'seq'}, dimensions={0}, use_global_device_ids=true | all-gather | bytes 327680 | tf_op jit(solution)/shard_map/all_gather | solution.py:90
  217.0 0.3 convolution_convert_fusion.3
  217.3 16.2 %all_gather.27 = bf16[8,32,1344]{2,1,0:T(8,128)(2,1)S(1)} all-gather(bf16[2,32,1344]{2,1,0:T(8,128)(2,1)} %param.27), channel_id=1, replica_groups=mesh['groups'=2,'seq'=4,'head'=2,'rep'=2] {'seq'}, dimensions={0}, use_global_device_ids=true | all-gather | bytes 860160 | tf_op jit(solution)/shard_map/all_gather | solution.py:91
  233.5 0.4 convolution_convert_fusion.1
  234.1 0.2 convolution_bitcast_fusion
  234.3 10.7 %psum.15 = bf16[512,32]{0,1:T(8,128)(2,1)S(1)} all-reduce(f32[512,32]{0,1:T(8,128)S(1)} %bitcast.142), channel_id=1, replica_groups=mesh['groups'=2,'seq'=4,'head'=2,'rep'=2] {'head','rep'}, use_global_device_ids=true, to_apply=%region_9.10 | all-reduce | flops 16384 | bytes 98304 | tf_op jit(solution)/shard_map/psum | solution.py:252
  245.0 0.7 fusion.29
  245.7 7.3 %fusion.27 = bf16[512,1344]{0,1:T(8,128)(2,1)} fusion(bf16[2048,1344]{0,1:T(8,128)(2,1)} %param.20, bf16[512,2048]{0,1:T(8,128)(2,1)} %all-gather.8.cloned.1.call-done, f32[4,168,8,128]{3,2,1,0:T(8,128)S(1)} %fusion.29), kind=kOutput, calls=%fused_computation.38 | convolution fusion | flops 2819948544 | bytes 11730944 | tf_op jit(solution)/shard_map/dot_general | solution.py:240
  (64 shorter events, 2.0 us)
Async XLA Ops:
  6.5 61.3 %all-gather.6.cloned.1.call-start = ((), (), s32[]{:S(2)}) async-start(), calls=%async_computation.1 | async-start | bytes 2703360 | tf_op jit(solution)/shard_map/all_gather | solution.py:87
  7.3 105.1 %all-gather.4.cloned.1.call-start = ((), (), s32[]{:S(2)}) async-start(), calls=%async_computation | async-start | bytes 6881280 | tf_op jit(solution)/shard_map/all_gather | solution.py:120
  8.0 62.4 %copy-start.2 = (bf16[512,1344]{0,1:T(8,128)(2,1)S(1)}, bf16[512,1344]{0,1:T(8,128)(2,1)}, u32[]{:S(2)}) copy-start(bf16[512,1344]{0,1:T(8,128)(2,1)} %param.16) | copy-start | bytes 4128772
  8.0 237.7 %all-gather.8.cloned.1.call-start = ((), (), s32[]{:S(2)}) async-start(), calls=%async_computation.2 | async-start | bytes 2621440 | tf_op jit(solution)/shard_map/all_gather | solution.py:241
  112.4 7.7 %copy-start.7 = (bf16[512,5376]{0,1:T(8,128)(2,1)S(1)}, bf16[512,5376]{0,1:T(8,128)(2,1)}, u32[]{:S(2)}) copy-start(bf16[512,5376]{0,1:T(8,128)(2,1)} %all-gather.4.cloned.1.call-done) | copy-start | bytes 16515076
  112.4 14.5 %slice-start = ((s8[5505024]{0:T(1024)(128)(4,1)}), s8[4194304]{0:T(1024)(128)(4,1)S(1)}, s32[]{:S(2)}) async-start(s8[5505024]{0:T(1024)(128)(4,1)} %bitcast.144), calls=%async_computation.3 | async-start | bytes 8388608
  120.0 5.3 %copy-start.5 = (f32[128]{0:T(128)S(1)}, f32[128]{0:T(128)}, u32[]{:S(2)}) copy-start(f32[128]{0:T(128)} %param.22) | copy-start | bytes 1540
  120.0 5.5 %copy-start.6 = (f32[128]{0:T(128)S(1)}, f32[128]{0:T(128)}, u32[]{:S(2)}) copy-start(f32[128]{0:T(128)} %param.21) | copy-start | bytes 1540
  120.0 6.8 %slice-start.1 = ((s8[5505024]{0:T(1024)(128)(4,1)}), s8[1310720]{0:T(1024)(128)(4,1)S(1)}, s32[]{:S(2)}) async-start(s8[5505024]{0:T(1024)(128)(4,1)} %bitcast.144), calls=%async_computation.4 | async-start | bytes 2621440
  130.2 5.3 %copy-start.1 = (bf16[1,512,256]{2,1,0:T(8,128)(2,1)}, bf16[1,512,256]{2,1,0:T(8,128)(2,1)S(1)}, u32[]{:S(2)}) copy-start(bf16[1,512,256]{2,1,0:T(8,128)(2,1)S(1)} %copy.115) | copy-start | bytes 786436
  131.1 16.2 %collective-permute-start = (bf16[2,512,256]{2,1,0:T(8,128)(2,1)}, bf16[2,512,256]{2,1,0:T(8,128)(2,1)}, u32[]{:S(2)}, u32[]{:S(2)}) collective-permute-start(bf16[2,512,256]{2,1,0:T(8,128)(2,1)} %pad_maximum_fusion), channel_id=1, source_target_pairs={{0,8},{4,12},{1,9},{5,13},{2,10},{6,14},{3,11},{7,15},{16,24},{20,... | collective-permute-start | bytes 1572872 | tf_op jit(solution)/shard_map/ppermute | solution.py:20
  135.5 22.4 %collective-permute-start.1 = (bf16[2,512,256]{2,1,0:T(8,128)(2,1)}, bf16[2,512,256]{2,1,0:T(8,128)(2,1)}, u32[]{:S(2)}, u32[]{:S(2)}) collective-permute-start(bf16[2,512,256]{2,1,0:T(8,128)(2,1)} %pad_maximum_fusion), channel_id=1, source_target_pairs={{0,4},{4,8},{8,12},{1,5},{5,9},{9,13},{2,6},{6,10},{10,14},{3,7},{... | collective-permute-start | bytes 1572872 | tf_op jit(solution)/shard_map/ppermute | solution.py:20
  159.3 0.7 copy-start.4
  159.9 30.6 %copy-start.3 = (bf16[2,512,32]{1,2,0:T(8,128)(2,1)S(1)}, bf16[2,512,32]{1,2,0:T(8,128)(2,1)}, u32[]{:S(2)}) copy-start(bf16[2,512,32]{1,2,0:T(8,128)(2,1)} %param.26) | copy-start | bytes 196612
  190.5 43.5 %copy-start = (bf16[512,2,2,128]{0,3,2,1:T(8,128)(2,1)S(1)}, bf16[512,2,2,128]{0,3,2,1:T(8,128)(2,1)}, u32[]{:S(2)}) copy-start(bf16[512,2,2,128]{0,3,2,1:T(8,128)(2,1)} %divide_convert_fusion) | copy-start | bytes 1572868
Sparse Core Ops, SparseCore 0:
  8.9 58.8 all-gather.5
  69.4 42.9 all-gather.3
  190.6 33.6 all-gather.7
where the time goes:
time: 260 us
  blocking collectives  111 us (43%)
  waiting for transfers between devices  54.1 us (21%)
  matrix products  51.5 us (20%)
  between operations  13.5 us (5%)
  other arithmetic  9.9 us (4%)
  local copies, waits for them, and re-layouts  9.48 us (4%)
  starting transfers between devices  8.35 us (3%)
    all_gather x1, blocking collectives, per_device(): lax.all_gather(adapter_out_down, 'seq', axis=0, tiled=True)  26.5 us
    all_gather x1, blocking collectives, per_device(): lax.all_gather(key_value_up_panels, 'seq', axis=0, tiled=True)  23.4 us
    all_gather x1, waiting for transfers between devices, per_device(): feature_part = lax.all_gather(tokens, ('head', 'rep'), axis=1, tiled=True)  21.5 us
    all_gather x1, blocking collectives, per_device(): lax.all_gather(adapter_up_query, 'seq', axis=0, tiled=True)  16.8 us
    psum x1, blocking collectives, per_device(): lax.psum(partial_low, ('head', 'rep')).astype(jnp.bfloat16)  16.8 us
    all_gather x1, blocking collectives, per_device(): lax.all_gather(adapter_out_up, 'seq', axis=0, tiled=True)  16.2 us
    ppermute x2, waiting for transfers between devices, shifted(): return lax.ppermute(value, axis, pairs)  15.6 us
    all_gather x1, waiting for transfers between devices, per_device(): lax.all_gather(adapter_down, 'seq', axis=0, tiled=True)  15.6 us
  transfers between devices with their start and end apart: 5, of which 4 were waited for; matrix products, arithmetic and copies ran while one was open for 6% of the time, Pallas kernels for 0%

commit v1 on v0

--- a/solution.py
+++ b/solution.py
@@ -249,7 +249,7 @@
         chosen_out_down,
         preferred_element_type=jnp.float32,
     ).reshape(tok_rows, ADAPTER_RANK)
-    output_reduced_rank = lax.psum(local_low, ("head", "rep")).astype(jnp.bfloat16)
+    output_reduced_rank = lax.psum(lax.psum(local_low, "rep"), "head").astype(jnp.bfloat16)
     result = projected_rows + adapter_scale * jnp.einsum(
         "zch,zhp->zcp",
         output_reduced_rank.reshape(block_count, BLOCK, ADAPTER_RANK),

time: 260 us -> 277 us (1.065)
  blocking collectives: 111 us -> 122 us
  local copies, waits for them, and re-layouts: 9.48 us -> 14.8 us
    ppermute x2, waiting for transfers between devices: 15.6 us -> 0.01 us  [shifted(): return lax.ppermute(value, axis, pairs)]
    all_gather x1, blocking collectives: 26.5 us -> 40.6 us  [per_device(): lax.all_gather(adapter_out_down, 'seq', axis=0, tiled=True)]
    all_gather x1, waiting for transfers between devices: 0.02 us -> 13.8 us  [per_device(): lax.all_gather(attention_result, ('head', 'rep'), axis=1, tiled=True)]
  transfers between devices with their start and end apart: 5 -> 6, of which waited for: 4 -> 3; matrix products, arithmetic and copies ran while one was open for 6% -> 5% of each run, Pallas kernels for 0% -> 0%
where the time goes in v1:
time: 277 us; the launch traced here: 276 us
  blocking collectives  122 us (44%)
  waiting for transfers between devices  52.6 us (19%)
  matrix products  51.5 us (19%)
  local copies, waits for them, and re-layouts  14.8 us (5%)
  between operations  13.6 us (5%)
  other arithmetic  11.2 us (4%)
  starting transfers between devices  8.46 us (3%)
    all_gather x1, blocking collectives, per_device(): lax.all_gather(adapter_out_down, 'seq', axis=0, tiled=True)  40.6 us
    all_gather x1, blocking collectives, per_device(): lax.all_gather(key_value_up_panels, 'seq', axis=0, tiled=True)  23.5 us
    all_gather x1, waiting for transfers between devices, per_device(): feature_part = lax.all_gather(tokens, ('head', 'rep'), axis=1, tiled=True)  21.6 us
    all_gather x1, blocking collectives, per_device(): lax.all_gather(adapter_up_query, 'seq', axis=0, tiled=True)  16.6 us
    psum x1, blocking collectives, per_device(): lax.psum(partial_low, ('head', 'rep')).astype(jnp.bfloat16)  16.5 us
    all_gather x1, blocking collectives, per_device(): lax.all_gather(adapter_out_up, 'seq', axis=0, tiled=True)  16.1 us
    all_gather x1, waiting for transfers between devices, per_device(): lax.all_gather(adapter_down, 'seq', axis=0, tiled=True)  15.2 us
    all_gather x1, waiting for transfers between devices, per_device(): lax.all_gather(attention_result, ('head', 'rep'), axis=1, tiled=True)  13.8 us
  transfers between devices with their start and end apart: 6, of which 3 were waited for; matrix products, arithmetic and copies ran while one was open for 5% of the time, Pallas kernels for 0%

profile of v1, /device:TPU:0, one launch (start us, length us, event | category | flops | bytes accessed | tf_op | source)
XLA Modules:
  0.0 276.3 jit_solution(6094794574586651887)
XLA Ops:
  6.5 0.7 all-gather.6.cloned.1.call-update
  7.3 0.7 all-gather.4.cloned.1.call-update
  8.1 1.4 dynamic_slice.29
  9.5 16.6 %all_gather.24 = bf16[8,32,512]{2,1,0:T(8,128)(2,1)S(1)} all-gather(bf16[2,32,512]{2,1,0:T(8,128)(2,1)} %param.24), channel_id=1, replica_groups=mesh['groups'=2,'seq'=4,'head'=2,'rep'=2] {'seq'}, dimensions={0}, use_global_device_ids=true | all-gather | bytes 327680 | tf_op jit(solution)/shard_map/all_gather | solution.py:88
  26.1 0.9 convert_reduce_fusion
  27.0 0.8 fusion.62
  27.7 23.5 %all_gather.23 = bf16[8,2,32,512]{3,2,1,0:T(8,128)(2,1)S(1)} all-gather(bf16[2,2,32,512]{3,2,1,0:T(8,128)(2,1)} %param.25), channel_id=1, replica_groups=mesh['groups'=2,'seq'=4,'head'=2,'rep'=2] {'seq'}, dimensions={0}, use_global_device_ids=true | all-gather | bytes 655360 | tf_op jit(solution)/shard_map/all_gather | solution.py:89
  51.4 0.5 multiply_cosine_fusion
  51.9 0.4 convolution_convert_fusion.2
  52.4 0.3 convolution_convert_fusion.4
  52.7 15.2 %all-gather.6.cloned.1.call-done = bf16[8,1344,96]{1,2,0:T(8,128)(2,1)} async-done(((bf16[2,1344,96]{1,2,0:T(8,128)(2,1)}), bf16[8,1344,96]{1,2,0:T(8,128)(2,1)}) %all-gather.6.cloned.1.call-update) | async-done | bytes 2064400 | tf_op jit(solution)/shard_map/all_gather | solution.py:87
  67.9 2.6 convolution_convert_fusion
  70.6 0.5 fusion.35
  71.1 16.5 %all-reduce.4 = bf16[512,96]{0,1:T(8,128)(2,1)S(1)} all-reduce(f32[512,96]{0,1:T(8,128)S(1)} %bitcast.140), channel_id=1, replica_groups=mesh['groups'=2,'seq'=4,'head'=2,'rep'=2] {'head','rep'}, use_global_device_ids=true, to_apply=%region_1.2 | all-reduce | flops 49152 | bytes 294912 | tf_op jit(solution)/shard_map/psum | solution.py:116
  87.6 0.3 convolution_multiply_fusion.3
  88.0 1.3 copy.113
  89.3 0.3 convolution_multiply_fusion.1
  89.6 0.3 copy.96
  90.0 0.3 convolution_multiply_fusion.2
  90.3 0.3 copy.91
  90.7 21.6 %all-gather.4.cloned.1.call-done = bf16[512,5376]{0,1:T(8,128)(2,1)} async-done(((bf16[512,1344]{0,1:T(8,128)(2,1)}), bf16[512,5376]{0,1:T(8,128)(2,1)}) %all-gather.4.cloned.1.call-update) | async-done | bytes 5505040 | tf_op jit(solution)/shard_map/all_gather | solution.py:120
  112.3 7.6 %fusion.39 = (f32[512,4]{0,1:T(4,128)S(1)}, bf16[512,512]{0,1:T(8,128)(2,1)S(1)}) fusion(f32[512,512]{0,1:T(8,128)} %copy.113, bf16[512,5376]{0,1:T(8,128)(2,1)} %all-gather.4.cloned.1.call-done, bf16[5376,512]{1,0:T(8,128)(2,1)} %param.18), kind=kOutput, calls=%fused_computation.63 | convolution fusion | flops 2819880960 | bytes 12591104 | tf_op jit(solution)/shard_map/dot_general | solution.py:122
  120.0 5.2 %multiply_reduce_fusion = (f32[512,4]{0,1:T(4,128)S(1)}, f32[512,512]{0,1:T(8,128)S(1)}) fusion(f32[512,512]{0,1:T(8,128)S(1)} %copy.96, bf16[512,5376]{0,1:T(8,128)(2,1)S(1)} %copy-done.10, bf16[5376,512]{1,0:T(8,128)(2,1)} %param.17), kind=kOutput, calls=%fused_computation.69 | convolution fusion | flops 2819356672 | bytes 13115392 | tf_op jit(solution)/shard_map/dot_general | solution.py:121
  125.6 1.1 multiply_subtract_fusion
  126.8 3.0 %fusion.34 = bf16[512,512]{0,1:T(8,128)(2,1)S(1)} fusion(f32[512,512]{0,1:T(8,128)S(1)} %copy.91, bf16[512,5376]{0,1:T(8,128)(2,1)S(1)} %copy-done.10, bf16[5376,512]{1,0:T(8,128)(2,1)S(1)} %bitcast.145), kind=kOutput, calls=%fused_computation.56 | convolution fusion | flops 2819096576 | bytes 12582912 | tf_op jit(solution)/shard_map/dot_general | solution.py:123
  130.2 0.9 pad_maximum_fusion
  131.1 4.5 %collective-permute-start = (bf16[2,512,256]{2,1,0:T(8,128)(2,1)}, bf16[2,512,256]{2,1,0:T(8,128)(2,1)}, u32[]{:S(2)}, u32[]{:S(2)}) collective-permute-start(bf16[2,512,256]{2,1,0:T(8,128)(2,1)} %pad_maximum_fusion), channel_id=1, source_target_pairs={{0,8},{4,12},{1,9},{5,13},{2,10},{6,14},{3,11},{7,15},{16,24},{20,... | collective-permute-start | bytes 1572872 | tf_op jit(solution)/shard_map/ppermute | solution.py:20
  135.6 3.8 %collective-permute-start.1 = (bf16[2,512,256]{2,1,0:T(8,128)(2,1)}, bf16[2,512,256]{2,1,0:T(8,128)(2,1)}, u32[]{:S(2)}, u32[]{:S(2)}) collective-permute-start(bf16[2,512,256]{2,1,0:T(8,128)(2,1)} %pad_maximum_fusion), channel_id=1, source_target_pairs={{0,4},{4,8},{8,12},{1,5},{5,9},{9,13},{2,6},{6,10},{10,14},{3,7},{... | collective-permute-start | bytes 1572872 | tf_op jit(solution)/shard_map/ppermute | solution.py:20
  139.5 40.6 %all_gather.26 = bf16[8,512,32]{1,2,0:T(8,128)(2,1)S(1)} all-gather(bf16[2,512,32]{1,2,0:T(8,128)(2,1)S(1)} %copy-done.4), channel_id=1, replica_groups=mesh['groups'=2,'seq'=4,'head'=2,'rep'=2] {'seq'}, dimensions={0}, use_global_device_ids=true | all-gather | bytes 327680 | tf_op jit(solution)/shard_map/all_gather | solution.py:90
  180.4 0.3 copy.97
  180.7 1.4 copy.98
  182.1 1.1 fusion.41
  183.3 1.4 maximum_maximum_fusion
  185.1 0.5 iota.44
  185.7 35.2 %while.15 = (s32[]{:T(128)}, f32[512,2,2,128]{0,3,2,1:T(8,128)S(1)}, f32[2,2,512]{2,1,0:T(2,128)S(1)}, bf16[3,512,2,128]{3,2,1,0:T(2,128)(2,1)S(1)}, s32[3]{0:T(...) while((s32[]{:T(128)}, ...), condition=%wide.region_8.9_spmd.clone, body=%wide.region_5.8_spmd.clone.sunk | while | flops 543460864 | bytes 13948180 | solution.py:227
  185.7 1.2 dynamic_slice.49
  187.5 0.7 select_reduce_fusion.2
  188.3 0.7 broadcast_bitcast_fusion.2
  189.0 0.5 fusion.92
  189.5 0.4 constant_dynamic-slice_fusion.4
  189.9 4.0 %fusion.93 = (f32[2,2,512]{2,1,0:T(2,128)S(1)}, f32[2,512,512,2]{2,1,3,0:T(8,128)}) fusion(pred[512,512]{0,1:T(8,128)(4,1)S(1)} %fusion.92, bf16[512,2,2,128]{3,0,2,1:T(8,128)(2,1)} %get-tuple-element.399, bf16[1,512,2,128]{3,2,1,0:T(2,128)(2,1)S(1)} %get-tuple-element.359), kind=kOutput, calls=%fused_computation.4.clone.1 | convolution fusion | flops 270530560 | bytes 5251072 | tf_op jit(solution)/shard_map/while/body/eval_jaxpr/tcpd,kcd->cptk/dot_general | solution.py:213
  194.1 3.2 %fusion.94 = f32[512,2,2,128]{0,3,2,1:T(8,128)S(1)} fusion(f32[2,512,512,2]{2,1,3,0:T(8,128)} %get-tuple-element.360, pred[512,512]{0,1:T(8,128)(4,1)S(1)} %fusion.92, f32[512,2,2,128]{0,3,2,1:T(8,128)S(1)} %get-tuple-element.378, pred[]{:T(512)S(6)} %compare.16, bf16[1,512,2,128]{1,3,2,0:T(8,128)(2,1)S(1)} %copy.178), kind=kOutput, calls=%fused_computation.12.clone.1 | convolution fusion | flops 271056896 | bytes 6815745 | tf_op jit(solution)/shard_map/while/body/eval_jaxpr/cptk,kcd->tcpd/dot_general | solution.py:219
  197.4 1.2 dynamic_slice.49
  199.3 0.7 select_reduce_fusion.2
  200.0 0.7 broadcast_bitcast_fusion.2
  200.7 0.5 fusion.92
  201.2 0.4 constant_dynamic-slice_fusion.4
  201.6 4.1 %fusion.93 = (f32[2,2,512]{2,1,0:T(2,128)S(1)}, f32[2,512,512,2]{2,1,3,0:T(8,128)}) fusion(pred[512,512]{0,1:T(8,128)(4,1)S(1)} %fusion.92, bf16[512,2,2,128]{3,0,2,1:T(8,128)(2,1)} %get-tuple-element.399, bf16[1,512,2,128]{3,2,1,0:T(2,128)(2,1)S(1)} %get-tuple-element.359), kind=kOutput, calls=%fused_computation.4.clone.1 | convolution fusion | flops 270530560 | bytes 5251072 | tf_op jit(solution)/shard_map/while/body/eval_jaxpr/tcpd,kcd->cptk/dot_general | solution.py:213
  205.8 3.2 %fusion.94 = f32[512,2,2,128]{0,3,2,1:T(8,128)S(1)} fusion(f32[2,512,512,2]{2,1,3,0:T(8,128)} %get-tuple-element.360, pred[512,512]{0,1:T(8,128)(4,1)S(1)} %fusion.92, f32[512,2,2,128]{0,3,2,1:T(8,128)S(1)} %get-tuple-element.378, pred[]{:T(512)S(6)} %compare.16, bf16[1,512,2,128]{1,3,2,0:T(8,128)(2,1)S(1)} %copy.178), kind=kOutput, calls=%fused_computation.12.clone.1 | convolution fusion | flops 271056896 | bytes 6815745 | tf_op jit(solution)/shard_map/while/body/eval_jaxpr/cptk,kcd->tcpd/dot_general | solution.py:219
  209.1 1.2 dynamic_slice.49
  211.0 0.7 select_reduce_fusion.2
  211.8 0.7 broadcast_bitcast_fusion.2
  212.5 0.5 fusion.92
  213.0 0.4 constant_dynamic-slice_fusion.4
  213.4 4.1 %fusion.93 = (f32[2,2,512]{2,1,0:T(2,128)S(1)}, f32[2,512,512,2]{2,1,3,0:T(8,128)}) fusion(pred[512,512]{0,1:T(8,128)(4,1)S(1)} %fusion.92, bf16[512,2,2,128]{3,0,2,1:T(8,128)(2,1)} %get-tuple-element.399, bf16[1,512,2,128]{3,2,1,0:T(2,128)(2,1)S(1)} %get-tuple-element.359), kind=kOutput, calls=%fused_computation.4.clone.1 | convolution fusion | flops 270530560 | bytes 5251072 | tf_op jit(solution)/shard_map/while/body/eval_jaxpr/tcpd,kcd->cptk/dot_general | solution.py:213
  217.6 3.2 %fusion.94 = f32[512,2,2,128]{0,3,2,1:T(8,128)S(1)} fusion(f32[2,512,512,2]{2,1,3,0:T(8,128)} %get-tuple-element.360, pred[512,512]{0,1:T(8,128)(4,1)S(1)} %fusion.92, f32[512,2,2,128]{0,3,2,1:T(8,128)S(1)} %get-tuple-element.378, pred[]{:T(512)S(6)} %compare.16, bf16[1,512,2,128]{1,3,2,0:T(8,128)(2,1)S(1)} %copy.178), kind=kOutput, calls=%fused_computation.12.clone.1 | convolution fusion | flops 271056896 | bytes 6815745 | tf_op jit(solution)/shard_map/while/body/eval_jaxpr/cptk,kcd->tcpd/dot_general | solution.py:219
  221.4 0.6 copy.174
  222.1 0.5 all-gather.8.cloned.1.call-update
  222.6 16.1 %all_gather.27 = bf16[8,32,1344]{2,1,0:T(8,128)(2,1)S(1)} all-gather(bf16[2,32,1344]{2,1,0:T(8,128)(2,1)S(1)} %copy-done.3), channel_id=1, replica_groups=mesh['groups'=2,'seq'=4,'head'=2,'rep'=2] {'seq'}, dimensions={0}, use_global_device_ids=true | all-gather | bytes 860160 | tf_op jit(solution)/shard_map/all_gather | solution.py:91
  238.7 0.4 convolution_convert_fusion.1
  239.2 8.8 %psum.23 = bf16[512,32]{0,1:T(8,128)(2,1)S(1)} all-reduce(f32[512,32]{0,1:T(8,128)} %all-reduce.3.cloned.1.call-done), channel_id=1, replica_groups=mesh['groups'=2,'seq'=4,'head'=2,'rep'=2] {'head'}, use_global_device_ids=true, to_apply=%region_10.11 | all-reduce | flops 16384 | bytes 98304 | tf_op jit(solution)/shard_map/psum | solution.py:252
  247.9 0.7 fusion.29
  248.6 13.8 %all-gather.8.cloned.1.call-done = bf16[512,2048]{0,1:T(8,128)(2,1)} async-done(((bf16[512,512]{0,1:T(8,128)(2,1)}), bf16[512,2048]{0,1:T(8,128)(2,1)}) %all-gather.8.cloned.1.call-update) | async-done | bytes 2097168 | tf_op jit(solution)/shard_map/all_gather | solution.py:241
  262.5 7.3 %fusion.27 = bf16[512,1344]{0,1:T(8,128)(2,1)} fusion(bf16[2048,1344]{0,1:T(8,128)(2,1)} %param.20, bf16[512,2048]{0,1:T(8,128)(2,1)} %all-gather.8.cloned.1.call-done, f32[4,168,8,128]{3,2,1,0:T(8,128)S(1)} %fusion.29), kind=kOutput, calls=%fused_computation.38 | convolution fusion | flops 2819948544 | bytes 11730944 | tf_op jit(solution)/shard_map/dot_general | solution.py:240
  (73 shorter events, 3.0 us)
Async XLA Ops:
  6.5 61.4 %all-gather.6.cloned.1.call-start = ((), (), s32[]{:S(2)}) async-start(), calls=%async_computation.1 | async-start | bytes 2703360 | tf_op jit(solution)/shard_map/all_gather | solution.py:87
  7.3 105.1 %all-gather.4.cloned.1.call-start = ((), (), s32[]{:S(2)}) async-start(), calls=%async_computation | async-start | bytes 6881280 | tf_op jit(solution)/shard_map/all_gather | solution.py:120
  8.0 62.5 %copy-start.2 = (bf16[512,1344]{0,1:T(8,128)(2,1)S(1)}, bf16[512,1344]{0,1:T(8,128)(2,1)}, u32[]{:S(2)}) copy-start(bf16[512,1344]{0,1:T(8,128)(2,1)} %param.16) | copy-start | bytes 4128772
  8.0 231.1 %all-reduce.3.cloned.1.call-start = ((), (), s32[]{:S(2)}) async-start(), calls=%async_computation.3 | async-start | bytes 131072 | tf_op jit(solution)/shard_map/psum | solution.py:252
  27.7 40.2 %copy-start.5 = (s32[4]{0:T(128)}, s32[4]{0:T(128)S(1)}, u32[]{:S(2)}) copy-start(s32[4]{0:T(128)S(1)} %fusion.62) | copy-start | bytes 52
  112.3 7.7 %copy-start.10 = (bf16[512,5376]{0,1:T(8,128)(2,1)S(1)}, bf16[512,5376]{0,1:T(8,128)(2,1)}, u32[]{:S(2)}) copy-start(bf16[512,5376]{0,1:T(8,128)(2,1)} %all-gather.4.cloned.1.call-done) | copy-start | bytes 16515076
  112.3 14.4 %slice-start = ((s8[5505024]{0:T(1024)(128)(4,1)}), s8[4194304]{0:T(1024)(128)(4,1)S(1)}, s32[]{:S(2)}) async-start(s8[5505024]{0:T(1024)(128)(4,1)} %bitcast.144), calls=%async_computation.4 | async-start | bytes 8388608
  120.0 5.3 %copy-start.8 = (f32[128]{0:T(128)S(1)}, f32[128]{0:T(128)}, u32[]{:S(2)}) copy-start(f32[128]{0:T(128)} %param.22) | copy-start | bytes 1540
  120.0 5.5 %copy-start.9 = (f32[128]{0:T(128)S(1)}, f32[128]{0:T(128)}, u32[]{:S(2)}) copy-start(f32[128]{0:T(128)} %param.21) | copy-start | bytes 1540
  120.0 6.8 %slice-start.1 = ((s8[5505024]{0:T(1024)(128)(4,1)}), s8[1310720]{0:T(1024)(128)(4,1)S(1)}, s32[]{:S(2)}) async-start(s8[5505024]{0:T(1024)(128)(4,1)} %bitcast.144), calls=%async_computation.5 | async-start | bytes 2621440
  129.8 9.7 %copy-start.4 = (bf16[2,512,32]{1,2,0:T(8,128)(2,1)S(1)}, bf16[2,512,32]{1,2,0:T(8,128)(2,1)}, u32[]{:S(2)}) copy-start(bf16[2,512,32]{1,2,0:T(8,128)(2,1)} %param.26) | copy-start | bytes 196612
  129.8 50.3 %copy-start.6 = (s32[4]{0:T(128)S(1)}, s32[4]{0:T(128)}, u32[]{:S(2)}) copy-start(s32[4]{0:T(128)} %copy-done.5) | copy-start | bytes 52
  130.2 5.5 %copy-start.1 = (bf16[1,512,256]{2,1,0:T(8,128)(2,1)}, bf16[1,512,256]{2,1,0:T(8,128)(2,1)S(1)}, u32[]{:S(2)}) copy-start(bf16[1,512,256]{2,1,0:T(8,128)(2,1)S(1)} %copy.115) | copy-start | bytes 786436
  131.1 52.1 %collective-permute-start = (bf16[2,512,256]{2,1,0:T(8,128)(2,1)}, bf16[2,512,256]{2,1,0:T(8,128)(2,1)}, u32[]{:S(2)}, u32[]{:S(2)}) collective-permute-start(bf16[2,512,256]{2,1,0:T(8,128)(2,1)} %pad_maximum_fusion), channel_id=1, source_target_pairs={{0,8},{4,12},{1,9},{5,13},{2,10},{6,14},{3,11},{7,15},{16,24},{20,... | collective-permute-start | bytes 1572872 | tf_op jit(solution)/shard_map/ppermute | solution.py:20
  135.6 47.6 %collective-permute-start.1 = (bf16[2,512,256]{2,1,0:T(8,128)(2,1)}, bf16[2,512,256]{2,1,0:T(8,128)(2,1)}, u32[]{:S(2)}, u32[]{:S(2)}) collective-permute-start(bf16[2,512,256]{2,1,0:T(8,128)(2,1)} %pad_maximum_fusion), channel_id=1, source_target_pairs={{0,4},{4,8},{8,12},{1,5},{5,9},{9,13},{2,6},{6,10},{10,14},{3,7},{... | collective-permute-start | bytes 1572872 | tf_op jit(solution)/shard_map/ppermute | solution.py:20
  220.9 1.7 copy-start.3
  220.9 17.8 %copy-start.7 = (s32[4]{0:T(128)S(1)}, s32[4]{0:T(128)}, u32[]{:S(2)}) copy-start(s32[4]{0:T(128)} %copy-done.5) | copy-start | bytes 52
  221.0 1.1 copy-start
  222.0 40.4 %all-gather.8.cloned.1.call-start = ((), (), s32[]{:S(2)}) async-start(), calls=%async_computation.2 | async-start | bytes 2621440 | tf_op jit(solution)/shard_map/all_gather | solution.py:241
Sparse Core Ops, SparseCore 0:
  8.9 58.9 all-gather.5
  69.5 42.7 all-gather.3
  222.1 15.0 all-reduce.2
  238.7 23.7 all-gather.7
